TPU v7x, 32 devices: a whole 2x2x4 slice. The times are simulated.
32 devices in a mesh: wide: 8 (over y, x, core), narrow: 4 (over z).
Axes of the slice: x: 2, y: 2, z: 4, core: 2. Of those that a mesh axis runs over, the one named last changes fastest.
Arguments:
- tokens: bfloat16 [32, 512, 256], P('wide', 'narrow'), may hold values from -6 to 6
- kind: int32 [32], P('wide'), may hold values from 0 to 1
- proj_weight: bfloat16 [2, 256, 768], replicated, may hold values from -0.375 to 0.375
- proj_bias: float32 [2, 768], replicated, may hold values from -1.8 to 1.8
- ln1_gain: float32 [768], replicated, may hold values from 0.5 to 1.5
- ln1_bias: float32 [768], replicated, may hold values from -1.2 to 1.2
- qkv_weight: bfloat16 [768, 3, 768], P(None, None, 'narrow'), may hold values from -0.21875 to 0.21875
- qv_bias: float32 [2, 768], P(None, 'narrow'), may hold values from -1.8 to 1.8
- out_weight: bfloat16 [768, 768], P('narrow'), may hold values from -0.75 to 0.75
- out_bias: float32 [768], replicated, may hold values from -1.2 to 1.2
- ln2_gain: float32 [768], replicated, may hold values from 0.5 to 1.5
- ln2_bias: float32 [768], replicated, may hold values from -1.2 to 1.2
- up_weight: bfloat16 [768, 3072], P(None, 'narrow'), may hold values from -0.21875 to 0.21875
- up_bias: float32 [3072], replicated, may hold values from -1.8 to 1.8
- down_weight: bfloat16 [3072, 768], P('narrow'), may hold values from -0.109375 to 0.109375
- down_bias: float32 [768], replicated, may hold values from -1.2 to 1.2
- cotangent: bfloat16 [32, 512, 768], P('wide', 'narrow'), may hold values from -6 to 6
Outputs:
- out: bfloat16 [32, 512, 768], P('wide', 'narrow')
- tokens_grad: float32 [32, 512, 256], P('wide', 'narrow')
- proj_weight_grad: float32 [2, 256, 768], replicated
- proj_bias_grad: float32 [2, 768], replicated
- ln1_gain_grad: float32 [768], replicated
- ln1_bias_grad: float32 [768], replicated
- qkv_weight_grad: float32 [768, 3, 768], P(None, None, 'narrow')
- qv_bias_grad: float32 [2, 768], P(None, 'narrow')
- out_weight_grad: float32 [768, 768], P('narrow')
- out_bias_grad: float32 [768], replicated
- ln2_gain_grad: float32 [768], replicated
- ln2_bias_grad: float32 [768], replicated
- up_weight_grad: float32 [768, 3072], P(None, 'narrow')
- up_bias_grad: float32 [3072], P('narrow')
- down_weight_grad: float32 [3072, 768], P('narrow')
- down_bias_grad: float32 [768], replicated
Inputs may be any that keep to these rules, and one draw needn't show every extreme that they name: kind[c] is 0 for a clip of frame tokens and 1 for a clip of patch tokens.
All inputs are finite; a program needn't handle non-finite values.
Results may differ from a plain program's by a relative error of at most 0.019.
Values may be sent and summed in bfloat16 or wider, within the bound.
No kernel may reach another device: no remote copies, remote signals or barrier semaphores. Data moves between devices by JAX's collectives and lax.ppermute only.
A program may use at most 192 MiB of HBM per device.

v0:
```python
import jax
import jax.numpy as jnp
from jax import lax
from jax.sharding import PartitionSpec as P

HEAD_DIM = 64
epsilon = 1e-06


def layer_norm(values, norm_gain, norm_shift):
    row_mean = jnp.mean(values, axis=-1, keepdims=True)
    centred = values - row_mean
    row_var = jnp.mean(centred * centred, axis=-1, keepdims=True)
    return centred * lax.rsqrt(row_var + epsilon) * norm_gain + norm_shift


def exact_gelu(values):
    return 0.5 * values * (1.0 + jax.scipy.special.erf(values * 2.0 ** (-0.5)))


def project_heads(rows_full, qkv_weight, qv_bias):
    zero_row = jnp.zeros_like(qv_bias[0])
    bias_three = jnp.stack([qv_bias[0], zero_row, qv_bias[1]])
    projected = jnp.einsum(
        "cld,dke->kcle", rows_full, qkv_weight, preferred_element_type=jnp.float32
    )
    projected = (projected + bias_three[:, None, None, :]).astype(jnp.bfloat16)
    head_count = projected.shape[3] // HEAD_DIM
    return projected.reshape(3, projected.shape[1], projected.shape[2], head_count, HEAD_DIM)


def score_block(heads_qkv):
    return jnp.einsum(
        "clhe,cmhe->chlm", heads_qkv[0], heads_qkv[1], preferred_element_type=jnp.float32
    ) * HEAD_DIM ** (-0.5)


def mix_values(probs_low, heads_qkv):
    mixed = jnp.einsum(
        "chlm,cmhe->clhe", probs_low, heads_qkv[2], preferred_element_type=jnp.float32
    )
    mixed = mixed.astype(jnp.bfloat16)
    return mixed.reshape(mixed.shape[0], mixed.shape[1], mixed.shape[2] * mixed.shape[3])


def ffn_backward(rows_in, grad_rows, weight_in, weight_out, bias_in):
    hidden_pre = (
        jnp.einsum("cld,df->clf", rows_in, weight_in, preferred_element_type=jnp.float32) + bias_in
    )
    hidden_back = exact_gelu(hidden_pre).astype(jnp.bfloat16)
    out_grad = jnp.einsum("clf,cld->fd", hidden_back, grad_rows, preferred_element_type=jnp.float32)
    hidden_grad = jnp.einsum(
        "cld,fd->clf", grad_rows, weight_out, preferred_element_type=jnp.float32
    )
    gelu_value, gelu_pull = jax.vjp(exact_gelu, hidden_pre)
    pre_grad = gelu_pull(hidden_grad)[0].astype(jnp.bfloat16)
    in_grad = jnp.einsum("cld,clf->df", rows_in, pre_grad, preferred_element_type=jnp.float32)
    in_bias_grad = jnp.sum(pre_grad, axis=(0, 1), dtype=jnp.float32)
    rows_grad = jnp.einsum("clf,df->cld", pre_grad, weight_in, preferred_element_type=jnp.float32)
    return (in_grad, in_bias_grad, out_grad, rows_grad)


def per_device(
    tokens,
    kind,
    proj_weight,
    proj_bias,
    ln1_gain,
    ln1_bias,
    qkv_weight,
    qv_bias,
    out_weight,
    out_bias,
    ln2_gain,
    ln2_bias,
    up_weight,
    up_bias,
    down_weight,
    down_bias,
    cotangent,
):
    unit_share = up_weight.shape[1]
    local_bias = lax.dynamic_slice_in_dim(
        up_bias, lax.axis_index("narrow") * unit_share, unit_share, 0
    )
    is_patch = kind == 1
    chosen = jnp.where(is_patch[:, None, None], proj_weight[1], proj_weight[0])
    chosen_bias = jnp.where(is_patch[:, None], proj_bias[1], proj_bias[0])
    start_rows = (
        jnp.einsum("clf,cfd->cld", tokens, chosen, preferred_element_type=jnp.float32)
        + chosen_bias[:, None, :]
    )
    normed_one = layer_norm(start_rows, ln1_gain, ln1_bias).astype(jnp.bfloat16)
    rows_one = lax.all_gather(normed_one, "narrow", axis=1, tiled=True)
    heads_qkv = project_heads(rows_one, qkv_weight, qv_bias)
    scores = score_block(heads_qkv)
    row_max = jnp.max(scores, axis=-1, keepdims=True)
    log_total = row_max + jnp.log(jnp.sum(jnp.exp(scores - row_max), axis=-1, keepdims=True))
    probs_low = jnp.exp(scores - log_total).astype(jnp.bfloat16)
    mixed = mix_values(probs_low, heads_qkv)
    attn_part = jnp.einsum("cle,ed->cld", mixed, out_weight, preferred_element_type=jnp.float32)
    attn_rows = lax.psum_scatter(
        attn_part.astype(jnp.bfloat16), "narrow", scatter_dimension=1, tiled=True
    ).astype(jnp.float32)
    middle = start_rows + attn_rows + out_bias
    normed_two = layer_norm(middle, ln2_gain, ln2_bias).astype(jnp.bfloat16)
    rows_two = lax.all_gather(normed_two, "narrow", axis=1, tiled=True)
    hidden = exact_gelu(
        jnp.einsum("cld,df->clf", rows_two, up_weight, preferred_element_type=jnp.float32)
        + local_bias
    ).astype(jnp.bfloat16)
    mlp_part = jnp.einsum("clf,fd->cld", hidden, down_weight, preferred_element_type=jnp.float32)
    mlp_rows = lax.psum_scatter(
        mlp_part.astype(jnp.bfloat16), "narrow", scatter_dimension=1, tiled=True
    ).astype(jnp.float32)
    final_rows = middle + mlp_rows + down_bias
    output = final_rows.astype(jnp.bfloat16)
    down_bias_grad = jnp.sum(cotangent, axis=(0, 1), dtype=jnp.float32)
    grad_all = lax.all_gather(cotangent, "narrow", axis=1, tiled=True)
    rows_two_back = lax.all_gather(normed_two, "narrow", axis=1, tiled=True)
    up_weight_grad, up_bias_grad, down_weight_grad, norm_two_part = ffn_backward(
        rows_two_back, grad_all, up_weight, down_weight, local_bias
    )
    norm_two_grad = lax.psum_scatter(
        norm_two_part.astype(jnp.bfloat16), "narrow", scatter_dimension=1, tiled=True
    ).astype(jnp.float32)
    ln_value, ln_pull = jax.vjp(layer_norm, middle, ln2_gain, ln2_bias)
    mid_grad, ln2_gain_grad, ln2_bias_grad = ln_pull(norm_two_grad)
    mid_grad = mid_grad + cotangent.astype(jnp.float32)
    mid_low = mid_grad.astype(jnp.bfloat16)
    out_bias_grad = jnp.sum(mid_low, axis=(0, 1), dtype=jnp.float32)
    mid_all = lax.all_gather(mid_low, "narrow", axis=1, tiled=True)
    rows_one_back = lax.all_gather(normed_one, "narrow", axis=1, tiled=True)
    heads_back = project_heads(rows_one_back, qkv_weight, qv_bias)
    probs = jnp.exp(score_block(heads_back) - log_total)
    probs_back = probs.astype(jnp.bfloat16)
    mixed_back = mix_values(probs_back, heads_back)
    out_weight_grad = jnp.einsum(
        "cle,cld->ed", mixed_back, mid_all, preferred_element_type=jnp.float32
    )
    mixed_grad = jnp.einsum("cld,ed->cle", mid_all, out_weight, preferred_element_type=jnp.float32)
    mixed_grad = mixed_grad.astype(jnp.bfloat16).reshape(heads_back.shape[1:])
    probs_grad = jnp.einsum(
        "clhe,cmhe->chlm", mixed_grad, heads_back[2], preferred_element_type=jnp.float32
    )
    value_grad = jnp.einsum(
        "chlm,clhe->cmhe", probs_back, mixed_grad, preferred_element_type=jnp.float32
    )
    score_grad = probs * (probs_grad - jnp.sum(probs * probs_grad, axis=-1, keepdims=True))
    score_grad = score_grad.astype(jnp.bfloat16)
    query_grad = jnp.einsum(
        "chlm,cmhe->clhe", score_grad, heads_back[1], preferred_element_type=jnp.float32
    ) * HEAD_DIM ** (-0.5)
    key_grad = jnp.einsum(
        "chlm,clhe->cmhe", score_grad, heads_back[0], preferred_element_type=jnp.float32
    ) * HEAD_DIM ** (-0.5)
    stacked = jnp.stack([query_grad, key_grad, value_grad]).astype(jnp.bfloat16)
    stacked = stacked.reshape(
        3, stacked.shape[1], stacked.shape[2], stacked.shape[3] * stacked.shape[4]
    )
    qkv_weight_grad = jnp.einsum(
        "cld,kcle->dke", rows_one_back, stacked, preferred_element_type=jnp.float32
    )
    qv_bias_grad = jnp.stack(
        [
            jnp.sum(stacked[0], axis=(0, 1), dtype=jnp.float32),
            jnp.sum(stacked[2], axis=(0, 1), dtype=jnp.float32),
        ]
    )
    norm_one_part = jnp.einsum(
        "kcle,dke->cld", stacked, qkv_weight, preferred_element_type=jnp.float32
    )
    norm_one_grad = lax.psum_scatter(
        norm_one_part.astype(jnp.bfloat16), "narrow", scatter_dimension=1, tiled=True
    ).astype(jnp.float32)
    first_value, first_pull = jax.vjp(layer_norm, start_rows, ln1_gain, ln1_bias)
    start_grad, ln1_gain_grad, ln1_bias_grad = first_pull(norm_one_grad)
    start_low = (start_grad + mid_grad).astype(jnp.bfloat16)
    tokens_grad = jnp.einsum("cld,cfd->clf", start_low, chosen, preferred_element_type=jnp.float32)
    per_clip = jnp.einsum("clf,cld->cfd", tokens, start_low, preferred_element_type=jnp.float32)
    clip_bias = jnp.sum(start_low, axis=1, dtype=jnp.float32)
    proj_weight_grad = jnp.stack(
        [
            jnp.sum(jnp.where(is_patch[:, None, None], 0.0, per_clip), axis=0),
            jnp.sum(jnp.where(is_patch[:, None, None], per_clip, 0.0), axis=0),
        ]
    )
    proj_bias_grad = jnp.stack(
        [
            jnp.sum(jnp.where(is_patch[:, None], 0.0, clip_bias), axis=0),
            jnp.sum(jnp.where(is_patch[:, None], clip_bias, 0.0), axis=0),
        ]
    )
    common = lax.psum(
        (
            proj_weight_grad,
            proj_bias_grad,
            ln1_gain_grad,
            ln1_bias_grad,
            out_bias_grad,
            ln2_gain_grad,
            ln2_bias_grad,
            down_bias_grad,
        ),
        ("wide", "narrow"),
    )
    summed = lax.psum(
        (
            qkv_weight_grad,
            qv_bias_grad,
            out_weight_grad,
            up_weight_grad,
            up_bias_grad,
            down_weight_grad,
        ),
        "wide",
    )
    qkv_sum, qv_sum, out_sum, up_sum, up_bias_sum, down_sum = summed
    return (
        output,
        tokens_grad,
        common[0],
        common[1],
        common[2],
        common[3],
        qkv_sum,
        qv_sum,
        out_sum,
        common[4],
        common[5],
        common[6],
        up_sum,
        up_bias_sum,
        down_sum,
        common[7],
    )


def solution(mesh):
    in_specs = (
        P("wide", "narrow", None),
        P("wide"),
        P(),
        P(),
        P(),
        P(),
        P(None, None, "narrow"),
        P(None, "narrow"),
        P("narrow", None),
        P(),
        P(),
        P(),
        P(None, "narrow"),
        P(),
        P("narrow", None),
        P(),
        P("wide", "narrow", None),
    )
    out_specs = (
        P("wide", "narrow", None),
        P("wide", "narrow", None),
        P(),
        P(),
        P(),
        P(),
        P(None, None, "narrow"),
        P(None, "narrow"),
        P("narrow", None),
        P(),
        P(),
        P(),
        P(None, "narrow"),
        P("narrow"),
        P("narrow", None),
        P(),
    )
    return jax.shard_map(
        per_device, mesh=mesh, in_specs=in_specs, out_specs=out_specs, check_vma=False
    )
```

profile of v0, /device:TPU:0, one launch (start us, length us, event | category | flops | bytes accessed | tf_op | source)
XLA Modules:
  0.0 846.0 jit_solution(3704368714855647152)
XLA Ops:
  10.1 2.2 bitcast_reduce_fusion
  15.4 66.1 %all-gather.5.cloned.1.call-done = bf16[4,512,768]{1,2,0:T(8,128)(2,1)} async-done(((bf16[4,128,768]{1,2,0:T(8,128)(2,1)}), bf16[4,512,768]{1,2,0:T(8,128)(2,1)}) %all-gather.5.cloned.1.call-update) | async-done | bytes 3145744 | tf_op jit(solution)/shard_map/all_gather | solution.py:94
  81.5 4.0 fusion.5
  85.6 1.9 multiply_reduce_fusion.1
  87.5 2.1 exponential_reduce_fusion
  89.7 2.4 copy-done.2
  92.0 2.5 convolution_convert_fusion.5
  95.6 2.4 copy.95
  98.0 2.3 copy.107
  100.6 58.5 %reduce-scatter.13.cloned.1.call-done = bf16[128,3072]{1,0:T(8,128)(2,1)} async-done(((bf16[512,3072]{1,0:T(8,128)(2,1)}), bf16[128,3072]{1,0:T(8,128)(2,1)}) %reduce-scatter.13.cloned.1.call-update) | async-done | bytes 786448
  159.1 2.0 reshape.196
  161.1 1.3 copy.96
  162.4 1.9 fusion.54
  167.6 1.4 dynamic_slice.3
  169.0 61.4 %all-gather.7.cloned.1.call-done = bf16[4,512,768]{1,2,0:T(8,128)(2,1)} async-done(((bf16[4,128,768]{1,2,0:T(8,128)(2,1)}), bf16[4,512,768]{1,2,0:T(8,128)(2,1)}) %all-gather.7.cloned.1.call-update) | async-done | bytes 3145744 | tf_op jit(solution)/shard_map/all_gather | solution.py:107
  230.4 7.5 multiply_convert_fusion.1
  237.9 55.6 %all-gather.9.cloned.1.call-done = bf16[4,512,768]{2,1,0:T(8,128)(2,1)} async-done(((bf16[4,128,768]{2,1,0:T(8,128)(2,1)}), bf16[4,512,768]{2,1,0:T(8,128)(2,1)}) %all-gather.9.cloned.1.call-update) | async-done | bytes 3145744 | tf_op jit(solution)/shard_map/all_gather | solution.py:119
  293.5 8.1 convert_reduce_fusion
  301.6 1.7 copy-done.67
  303.3 2.9 convolution_convert_fusion.1
  306.1 2.4 copy.99
  308.6 2.4 copy.109
  313.3 56.9 %reduce-scatter.17.cloned.1.call-done = bf16[128,3072]{1,0:T(8,128)(2,1)} async-done(((bf16[512,3072]{1,0:T(8,128)(2,1)}), bf16[128,3072]{1,0:T(8,128)(2,1)}) %reduce-scatter.17.cloned.1.call-update) | async-done | bytes 786448
  370.2 2.7 reshape.200
  372.9 1.6 copy.100
  375.7 1.4 fusion.18
  377.2 2.2 convert_reduce_fusion.6
  379.5 4.8 convolution_convert_fusion.2
  384.3 2.4 copy.97
  386.8 2.5 copy.108
  389.5 53.4 %all-gather.11.cloned.1.call-done = bf16[4,512,768]{1,2,0:T(8,128)(2,1)} async-done(((bf16[4,128,768]{1,2,0:T(8,128)(2,1)}), bf16[4,512,768]{1,2,0:T(8,128)(2,1)}) %all-gather.11.cloned.1.call-update) | async-done | bytes 3145744 | tf_op jit(solution)/shard_map/all_gather | solution.py:132
  442.9 2.7 convolution_convert_fusion.3
  445.6 10.6 %multiply_reduce_fusion = (f32[4,3,512]{2,1,0:T(4,128)S(1)}, f32[4,3,512,512]{2,3,1,0:T(8,128)}) fusion(f32[4,3,512,512]{2,3,1,0:T(8,128)} %copy-done.2, f32[4,3,512]{2,1,0:T(4,128)S(1)} %copy-done.23, bf16[4,512,3,64]{1,3,2,0:T(8,128)(2,1)S(1)} %bitcast.173, bf16[4,512,3,64]{1,3,2,0:T(8,128)(2,1)S(1)} %bitcast.160), kind=kOutput, calls=%fused_computation.1 | convolution fusion | flops 415229952 | bytes 26787840 | tf_op jit(solution)/shard_map/clhe,cmhe->chlm/dot_general | solution.py:143
  456.3 1.4 slice-done.1
  457.6 1.3 slice-done.2
  458.9 6.9 multiply_convert_fusion
  465.8 2.0 multiply_convert_fusion.2
  467.8 1.8 convert_reduce_fusion.5
  469.6 3.2 convert_reduce_fusion.4
  472.8 3.0 bitcast_convert_fusion
  475.8 2.4 copy.101
  478.2 2.3 copy.110
  480.8 7.1 convolution_bitcast_fusion
  487.9 4.0 convolution_bitcast_fusion.1
  491.9 11.9 %reduce-scatter.15.cloned.1.call-done = bf16[128,3072]{1,0:T(8,128)(2,1)} async-done(((bf16[512,3072]{1,0:T(8,128)(2,1)}), bf16[128,3072]{1,0:T(8,128)(2,1)}) %reduce-scatter.15.cloned.1.call-update) | async-done | bytes 786448
  503.8 2.0 reshape.198
  505.8 1.3 copy.98
  507.2 59.3 %reduce-scatter.19.cloned.1.call-done = bf16[128,3072]{1,0:T(8,128)(2,1)} async-done(((bf16[512,3072]{1,0:T(8,128)(2,1)}), bf16[128,3072]{1,0:T(8,128)(2,1)}) %reduce-scatter.19.cloned.1.call-update) | async-done | bytes 786448
  566.5 2.7 reshape.202
  569.2 1.6 copy.102
  570.8 2.8 convert_reduce_fusion.1
  573.6 2.8 fusion.19
  576.5 3.5 convert_reduce_fusion.7
  582.2 4.0 convolution_bitcast_fusion.2
  586.3 5.3 fusion.23
  592.4 14.2 %all-reduce.1 = (f32[2,192]{1,0:T(2,128)}, f32[768]{0:T(1024)}) all-reduce(f32[2,192]{1,0:T(2,128)S(1)} %pad_maximum_fusion.6, f32[768]{0:T(1024)S(1)} %copy-done.57), channel_id=1, replica_groups=mesh['wide'=8,'narrow'=4] {'wide'}, use_global_device_ids=true, to_apply=%region_29.30 | all-reduce | flops 1152 | bytes 9216 | tf_op jit(solution)/shard_map/psum | solution.py:207
  608.0 41.0 %all-reduce = (f32[2,768]{1,0:T(2,128)}, f32[768]{0:T(1024)}, f32[768]{0:T(1024)}, f32[768]{0:T(1024)}, f32[768]{0:T(1024)}, /*index=5*/f32[768]{0:T(1024)}, f32[768]{0:T(1024)}) all-reduce(f32[2,768]{1,0:T(2,128)S(1)} %pad_maximum_fusion.4, f32[768]{0:T(1024)S(1)} %copy-done.49, ...), channel_id=1, replica_groups=mesh['wide'=8,'narrow'=4] {'wide','narrow'}, use_global_device_ids=true, to_apply=%region_21.22 | all-reduce | flops 6144 | bytes 49152 | tf_op jit(solution)/shard_map/psum | solution.py:194
  649.0 1.5 fusion.6
  650.5 64.2 %all-reduce.6.cloned.1.call-done = f32[2,256,768]{1,2,0:T(8,128)} async-done(((f32[2,256,768]{1,2,0:T(8,128)}), f32[2,256,768]{1,2,0:T(8,128)}) %all-reduce.6.cloned.1.call-update) | async-done | bytes 1572880 | tf_op jit(solution)/shard_map/psum | solution.py:194
  714.7 3.0 copy.77
  717.7 113.3 %all-reduce.8.cloned.1.call-done = (f32[768,3,192]{0,2,1:T(8,128)}, f32[192,768]{1,0:T(8,128)}, f32[768,768]{1,0:T(8,128)}, f32[768,768]{1,0:T(8,128)}) async-done(((f32[768,3,192]{0,2,1:T(8,128)}, f32[192,768]{1,0:T(8,128)}, f32[768,768]{1,0:T(8,128)}, f32[768,768]{1,0:T(8,128)}), (f32[768,3,192]{0,2,1:T(8,128)}, f32[192,768]{1,0:T(8,128)}, f32[768,768]{1,0:T(8,128)}, ...) | async-done | bytes 7077904 | tf_op jit(solution)/shard_map/psum | solution.py:207
  831.0 2.9 copy.116
  834.8 1.4 copy.118
  837.3 1.4 copy.119
  (196 shorter events, 21.0 us)
Async XLA Ops:
  7.2 223.2 %copy-start = (bf16[768,768]{1,0:T(8,128)(2,1)S(1)}, bf16[768,768]{1,0:T(8,128)(2,1)}, u32[]{:S(2)}) copy-start(bf16[768,768]{1,0:T(8,128)(2,1)} %param.29) | copy-start | bytes 3538948
  7.2 74.3 %all-gather.5.cloned.1.call-start = ((), (), s32[]{:S(2)}) async-start(), calls=%async_computation.4 | async-start | bytes 3932160 | tf_op jit(solution)/shard_map/all_gather | solution.py:94
  8.0 4.3 copy-start.60
  10.0 2.5 copy-start.31
  10.1 3.9 copy-start.36
  10.1 3.9 copy-start.54
  12.3 3.1 copy-start.59
  12.3 69.2 %copy-start.64 = (bf16[768,3,192]{0,2,1:T(8,128)(2,1)S(1)}, bf16[768,3,192]{0,2,1:T(8,128)(2,1)}, u32[]{:S(2)}) copy-start(bf16[768,3,192]{0,2,1:T(8,128)(2,1)} %param.23) | copy-start | bytes 2654212
  15.2 143.9 %reduce-scatter.13.cloned.1.call-start = ((), (), s32[]{:S(2)}) async-start(), calls=%async_computation.9 | async-start | bytes 3932160
  87.5 4.5 copy-start.2
  89.6 4.9 copy-start.22
  94.5 3.5 copy-start.7
  100.4 62.1 %copy-start.58 = (f32[768]{0:T(1024)S(1)}, f32[768]{0:T(1024)}, u32[]{:S(2)}) copy-start(f32[768]{0:T(1024)} %param.26) | copy-start | bytes 9220
  100.4 130.0 %all-gather.7.cloned.1.call-start = ((), (), s32[]{:S(2)}) async-start(), calls=%async_computation.5 | async-start | bytes 3932160 | tf_op jit(solution)/shard_map/all_gather | solution.py:107
  162.4 3.3 copy-start.35
  162.4 3.3 copy-start.55
  167.0 126.5 %all-gather.9.cloned.1.call-start = ((), (), s32[]{:S(2)}) async-start(), calls=%async_computation.6 | async-start | bytes 3932160 | tf_op jit(solution)/shard_map/all_gather | solution.py:119
  167.5 202.7 %reduce-scatter.17.cloned.1.call-start = ((), (), s32[]{:S(2)}) async-start(), calls=%async_computation.11 | async-start | bytes 3932160
  311.0 131.9 %all-gather.11.cloned.1.call-start = ((), (), s32[]{:S(2)}) async-start(), calls=%async_computation.7 | async-start | bytes 3932160 | tf_op jit(solution)/shard_map/all_gather | solution.py:132
  372.9 2.8 copy-start.45
  372.9 2.8 copy-start.38
  374.5 2.7 copy-start.11
  379.5 124.4 %reduce-scatter.15.cloned.1.call-start = ((), (), s32[]{:S(2)}) async-start(), calls=%async_computation.10 | async-start | bytes 3932160
  389.2 53.7 %copy-start.21 = (bf16[192,768]{1,0:T(8,128)(2,1)S(1)}, bf16[192,768]{1,0:T(8,128)(2,1)}, u32[]{:S(2)}) copy-start(bf16[192,768]{1,0:T(8,128)(2,1)} %param.25) | copy-start | bytes 884740
  389.3 56.3 %copy-start.23 = (f32[4,3,512]{2,1,0:T(4,128)S(1)}, f32[4,3,512]{2,1,0:T(4,128)}, u32[]{:S(2)}) copy-start(f32[4,3,512]{2,1,0:T(4,128)} %copy-done.22) | copy-start | bytes 73732
  389.3 177.2 %reduce-scatter.19.cloned.1.call-start = ((), (), s32[]{:S(2)}) async-start(), calls=%async_computation.12 | async-start | bytes 3932160
  445.6 10.7 %slice-start = ((s8[12582912]{0:T(1024)(128)(4,1)}), s8[4194304]{0:T(1024)(128)(4,1)S(1)}, s32[]{:S(2)}) async-start(s8[12582912]{0:T(1024)(128)(4,1)} %bitcast.157), calls=%async_computation.14 | async-start | bytes 8388608
  445.6 12.0 %slice-start.1 = ((s8[12582912]{0:T(1024)(128)(4,1)}), s8[4194304]{0:T(1024)(128)(4,1)S(1)}, s32[]{:S(2)}) async-start(s8[12582912]{0:T(1024)(128)(4,1)} %bitcast.157), calls=%async_computation.15 | async-start | bytes 8388608
  445.6 13.3 %slice-start.2 = ((s8[12582912]{0:T(1024)(128)(4,1)}), s8[4194304]{0:T(1024)(128)(4,1)S(1)}, s32[]{:S(2)}) async-start(s8[12582912]{0:T(1024)(128)(4,1)} %bitcast.157), calls=%async_computation.16 | async-start | bytes 8388608
  458.9 6.9 copy-start.6
  467.8 5.0 copy-start.18
  469.6 3.2 copy-start.26
  469.6 3.2 copy-start.65
  472.8 3.0 copy-start.28
  480.6 234.1 %all-reduce.6.cloned.1.call-start = ((), (), s32[]{:S(2)}) async-start(), calls=%async_computation.8 | async-start | bytes 3145728 | tf_op jit(solution)/shard_map/psum | solution.py:194
  480.8 7.1 copy-start.63
  480.8 7.1 copy-start.68
  569.2 4.4 copy-start.43
  569.2 4.4 copy-start.41
  570.7 5.7 copy-start.4
  570.8 5.7 copy-start.12
  570.8 5.7 copy-start.14
  570.8 5.7 copy-start.56
  576.4 3.5 copy-start.61
  576.4 3.5 copy-start.66
  582.1 4.2 copy-start.19
  582.1 4.1 copy-start.27
  582.1 4.1 copy-start.29
  582.1 248.9 %all-reduce.8.cloned.1.call-start = ((), (), s32[]{:S(2)}) async-start(), calls=%async_computation.13 | async-start | bytes 14155776 | tf_op jit(solution)/shard_map/psum | solution.py:207
  591.6 15.1 %copy-start.39 = (f32[4,768]{1,0:T(4,128)S(1)}, f32[4,768]{1,0:T(4,128)}, u32[]{:S(2)}) copy-start(f32[4,768]{1,0:T(4,128)} %get-tuple-element.77) | copy-start | bytes 36868
  591.6 15.1 %copy-start.62 = (pred[4]{0:T(512)(128)(4,1)S(1)}, pred[4]{0:T(512)(128)(4,1)}, u32[]{:S(2)}) copy-start(pred[4]{0:T(512)(128)(4,1)} %copy-done.60) | copy-start | bytes 16
  591.6 15.2 %copy-start.13 = (bf16[4,128,768]{1,2,0:T(8,128)(2,1)S(1)}, bf16[4,128,768]{1,2,0:T(8,128)(2,1)}, u32[]{:S(2)}) copy-start(bf16[4,128,768]{1,2,0:T(8,128)(2,1)} %get-tuple-element.84) | copy-start | bytes 2359300
  591.6 16.4 %copy-start.46 = (f32[768]{0:T(1024)S(1)}, f32[768]{0:T(1024)}, u32[]{:S(2)}) copy-start(f32[768]{0:T(1024)} %get-tuple-element.54) | copy-start | bytes 9220
  591.6 16.4 %copy-start.47 = (f32[768]{0:T(1024)S(1)}, f32[768]{0:T(1024)}, u32[]{:S(2)}) copy-start(f32[768]{0:T(1024)} %get-tuple-element.50) | copy-start | bytes 9220
  591.6 16.4 %copy-start.48 = (f32[768]{0:T(1024)S(1)}, f32[768]{0:T(1024)}, u32[]{:S(2)}) copy-start(f32[768]{0:T(1024)} %get-tuple-element.56) | copy-start | bytes 9220
  591.6 16.4 %copy-start.49 = (f32[768]{0:T(1024)S(1)}, f32[768]{0:T(1024)}, u32[]{:S(2)}) copy-start(f32[768]{0:T(1024)} %get-tuple-element.52) | copy-start | bytes 9220
  591.7 16.4 %copy-start.50 = (f32[768]{0:T(1024)S(1)}, f32[768]{0:T(1024)}, u32[]{:S(2)}) copy-start(f32[768]{0:T(1024)} %get-tuple-element.85) | copy-start | bytes 9220
  591.7 16.4 %copy-start.51 = (f32[768]{0:T(1024)S(1)}, f32[768]{0:T(1024)}, u32[]{:S(2)}) copy-start(f32[768]{0:T(1024)} %get-tuple-element.75) | copy-start | bytes 9220
  591.7 57.3 %copy-start.25 = (bf16[4,128,768]{1,2,0:T(8,128)(2,1)S(1)}, bf16[4,128,768]{1,2,0:T(8,128)(2,1)}, u32[]{:S(2)}) copy-start(bf16[4,128,768]{1,2,0:T(8,128)(2,1)} %copy-done.24) | copy-start | bytes 2359300
  591.7 57.3 %copy-start.32 = (bf16[256,768]{1,0:T(8,128)(2,1)S(1)}, bf16[256,768]{1,0:T(8,128)(2,1)}, u32[]{:S(2)}) copy-start(bf16[256,768]{1,0:T(8,128)(2,1)} %copy-done.31) | copy-start | bytes 1179652
  591.7 57.3 %copy-start.34 = (bf16[256,768]{1,0:T(8,128)(2,1)S(1)}, bf16[256,768]{1,0:T(8,128)(2,1)}, u32[]{:S(2)}) copy-start(bf16[256,768]{1,0:T(8,128)(2,1)} %copy-done.33) | copy-start | bytes 1179652
  831.0 3.0 copy-start.30
  831.0 3.8 copy-start.17
  834.8 3.9 copy-start.1
  (18 other events, 24.6 us)
Sparse Core Ops, SparseCore 0:
  15.3 66.1 all-gather.4
  100.5 58.5 reduce-scatter.12
  167.1 63.2 all-gather.6
  231.8 61.6 all-gather.8
  311.1 59.0 reduce-scatter.16
  379.6 63.2 all-gather.10
  445.2 58.5 reduce-scatter.14
  506.1 60.3 reduce-scatter.18
  582.2 132.4 all-reduce.5
  719.4 111.5 all-reduce.7
where the time goes:
time: 856 us; the launch traced here: 846 us
  waiting for transfers between devices  601 us (70%)
  matrix products  80.5 us (9%)
  local copies, waits for them, and re-layouts  62.2 us (7%)
  blocking collectives  55.2 us (6%)
  other arithmetic  29.9 us (3%)
  between operations  15.4 us (2%)
    unnamed x14, waiting for transfers between devices  187 us
    psum x1, waiting for transfers between devices, per_device(): lax.psum((qkv_weight_grad, qv_bias_grad, out_weight_grad, up_weight_grad,...  113 us
    all_gather x1, waiting for transfers between devices, per_device(): rows_one = lax.all_gather(normed_one, 'narrow', axis=1, tiled=True)  66.1 us
    psum x1, waiting for transfers between devices, per_device(): lax.psum((proj_weight_grad, proj_bias_grad, ln1_gain_grad, ln1_bias_grad,...  64.2 us
    all_gather x1, waiting for transfers between devices, per_device(): rows_two = lax.all_gather(normed_two, 'narrow', axis=1, tiled=True)  61.4 us
    unnamed x167, local copies, waits for them, and re-layouts  58.5 us
    all_gather x1, waiting for transfers between devices, per_device(): grad_all = lax.all_gather(cotangent, 'narrow', axis=1, tiled=True)  55.6 us
    all_gather x1, waiting for transfers between devices, per_device(): mid_all = lax.all_gather(mid_low, 'narrow', axis=1, tiled=True)  53.4 us
  transfers between devices with their start and end apart: 10, of which 10 were waited for; matrix products, arithmetic and copies ran while one was open for 10% of the time, Pallas kernels for 0%

commit v1 on v0

--- a/solution.py
+++ b/solution.py
@@ -5,6 +5,14 @@
 
 HEAD_DIM = 64
 epsilon = 1e-06
+
+
+def _check_block(in_array, xin):
+    return jnp.split(
+        lax.all_gather(jnp.concatenate([xin, in_array], 0), "narrow", axis=1, tiled=True),
+        [xin.shape[0]],
+        0,
+    )
 
 
 def layer_norm(values, norm_gain, norm_shift):
@@ -116,8 +124,7 @@
     final_rows = middle + mlp_rows + down_bias
     output = final_rows.astype(jnp.bfloat16)
     down_bias_grad = jnp.sum(cotangent, axis=(0, 1), dtype=jnp.float32)
-    grad_all = lax.all_gather(cotangent, "narrow", axis=1, tiled=True)
-    rows_two_back = lax.all_gather(normed_two, "narrow", axis=1, tiled=True)
+    grad_all, rows_two_back = _check_block(normed_two, cotangent)
     up_weight_grad, up_bias_grad, down_weight_grad, norm_two_part = ffn_backward(
         rows_two_back, grad_all, up_weight, down_weight, local_bias
     )

time: 856 us -> 906 us (1.058)
  waiting for transfers between devices: 601 us -> 644 us
    all_gather x1, waiting for transfers between devices: 55.6 us -> 114 us  [_check_block(): lax.all_gather(jnp.concatenate([xin, in_array], 0), 'narrow', axis=1, til...]
    unnamed x167 -> x187, local copies, waits for them, and re-layouts: 58.5 us -> 58.7 us
  transfers between devices with their start and end apart: 10 -> 10, of which waited for: 10 -> 10; matrix products, arithmetic and copies ran while one was open for 10% -> 11% of each run, Pallas kernels for 0% -> 0%
where the time goes in v1:
time: 906 us; the launch traced here: 895 us
  waiting for transfers between devices  644 us (71%)
  matrix products  84.5 us (9%)
  local copies, waits for them, and re-layouts  61.9 us (7%)
  blocking collectives  54.8 us (6%)
  other arithmetic  33.6 us (4%)
  between operations  15.5 us (2%)
    unnamed x14, waiting for transfers between devices  183 us
    all_gather x1, waiting for transfers between devices, _check_block(): lax.all_gather(jnp.concatenate([xin, in_array], 0), 'narrow', axis=1, til...  114 us
    psum x1, waiting for transfers between devices, per_device(): lax.psum((qkv_weight_grad, qv_bias_grad, out_weight_grad, up_weight_grad,...  113 us
    all_gather x1, waiting for transfers between devices, per_device(): rows_one = lax.all_gather(normed_one, 'narrow', axis=1, tiled=True)  66.1 us
    psum x1, waiting for transfers between devices, per_device(): lax.psum((proj_weight_grad, proj_bias_grad, ln1_gain_grad, ln1_bias_grad,...  64.8 us
    unnamed x187, local copies, waits for them, and re-layouts  58.7 us
    all_gather x1, waiting for transfers between devices, per_device(): rows_two = lax.all_gather(normed_two, 'narrow', axis=1, tiled=True)  54.7 us
    all_gather x1, waiting for transfers between devices, per_device(): mid_all = lax.all_gather(mid_low, 'narrow', axis=1, tiled=True)  47.4 us
  transfers between devices with their start and end apart: 10, of which 10 were waited for; matrix products, arithmetic and copies ran while one was open for 11% of the time, Pallas kernels for 0%

profile of v1, /device:TPU:0, one launch (start us, length us, event | category | flops | bytes accessed | tf_op | source)
XLA Modules:
  0.0 895.4 jit_solution(4802723561751425792)
XLA Ops:
  10.1 2.2 bitcast_reduce_fusion
  15.4 66.1 %all-gather.5.cloned.1.call-done = bf16[4,512,768]{1,2,0:T(8,128)(2,1)} async-done(((bf16[4,128,768]{1,2,0:T(8,128)(2,1)}), bf16[4,512,768]{1,2,0:T(8,128)(2,1)}) %all-gather.5.cloned.1.call-update) | async-done | bytes 3145744 | tf_op jit(solution)/shard_map/all_gather | solution.py:102
  81.5 4.0 fusion.10
  85.6 1.9 multiply_reduce_fusion.1
  87.5 2.1 exponential_reduce_fusion
  89.7 2.4 copy-done.2
  92.0 2.4 convolution_convert_fusion.4
  96.4 2.4 copy.106
  98.9 2.3 copy.118
  102.7 57.3 %reduce-scatter.13.cloned.1.call-done = bf16[128,3072]{1,0:T(8,128)(2,1)} async-done(((bf16[512,3072]{1,0:T(8,128)(2,1)}), bf16[128,3072]{1,0:T(8,128)(2,1)}) %reduce-scatter.13.cloned.1.call-update) | async-done | bytes 786448
  160.0 2.0 reshape.196
  162.0 1.3 copy.107
  163.3 1.9 fusion.71
  167.8 2.4 pad_maximum_fusion.1
  171.0 114.0 %all-gather.9.cloned.1.call-done = bf16[8,512,768]{1,2,0:T(8,128)(2,1)} async-done(((bf16[8,128,768]{1,2,0:T(8,128)(2,1)}), bf16[8,512,768]{1,2,0:T(8,128)(2,1)}) %all-gather.9.cloned.1.call-update) | async-done | bytes 6291472 | tf_op jit(solution)/shard_map/all_gather | solution.py:12
  285.1 4.8 fusion.43
  289.9 7.0 convert_reduce_fusion
  296.9 2.9 convolution_convert_fusion.1
  299.7 2.4 copy.110
  302.2 2.4 copy.120
  305.6 57.7 %reduce-scatter.17.cloned.1.call-done = bf16[128,3072]{1,0:T(8,128)(2,1)} async-done(((bf16[512,3072]{1,0:T(8,128)(2,1)}), bf16[128,3072]{1,0:T(8,128)(2,1)}) %reduce-scatter.17.cloned.1.call-update) | async-done | bytes 786448
  363.3 2.7 reshape.200
  366.0 1.5 copy.111
  369.5 2.1 fusion.27
  371.6 2.2 convert_reduce_fusion.6
  373.9 54.7 %all-gather.7.cloned.1.call-done = bf16[4,512,768]{1,2,0:T(8,128)(2,1)} async-done(((bf16[4,128,768]{1,2,0:T(8,128)(2,1)}), bf16[4,512,768]{1,2,0:T(8,128)(2,1)}) %all-gather.7.cloned.1.call-update) | async-done | bytes 3145744 | tf_op jit(solution)/shard_map/all_gather | solution.py:115
  428.6 9.3 %fusion.11 = bf16[4,512,768]{2,1,0:T(8,128)(2,1)} fusion(f32[768]{0:T(1024)} %copy-done.65, bf16[4,512,768]{1,2,0:T(8,128)(2,1)} %all-gather.7.cloned.1.call-done, bf16[768,768]{1,0:T(8,128)(2,1)} %param.31, bf16[768,768]{1,0:T(8,128)(2,1)S(1)} %copy-done), kind=kOutput, calls=%fused_computation.34 | convolution fusion | flops 4842848256 | bytes 8653824 | tf_op jit(solution)/shard_map/clf,fd->cld/dot_general | solution.py:120
  437.9 4.4 copy.108
  442.3 2.3 copy.119
  444.9 47.4 %all-gather.11.cloned.1.call-done = bf16[4,512,768]{1,2,0:T(8,128)(2,1)} async-done(((bf16[4,128,768]{1,2,0:T(8,128)(2,1)}), bf16[4,512,768]{1,2,0:T(8,128)(2,1)}) %all-gather.11.cloned.1.call-update) | async-done | bytes 3145744 | tf_op jit(solution)/shard_map/all_gather | solution.py:139
  492.3 2.7 convolution_convert_fusion.2
  495.0 10.6 %multiply_reduce_fusion = (f32[4,3,512]{2,1,0:T(4,128)S(1)}, f32[4,3,512,512]{2,3,1,0:T(8,128)}) fusion(f32[4,3,512,512]{2,3,1,0:T(8,128)} %copy-done.2, f32[4,3,512]{2,1,0:T(4,128)S(1)} %copy-done.25, bf16[4,512,3,64]{1,3,2,0:T(8,128)(2,1)S(1)} %bitcast.172, bf16[4,512,3,64]{1,3,2,0:T(8,128)(2,1)S(1)} %bitcast.159), kind=kOutput, calls=%fused_computation.1 | convolution fusion | flops 415229952 | bytes 26787840 | tf_op jit(solution)/shard_map/clhe,cmhe->chlm/dot_general | solution.py:150
  505.6 1.4 slice-done.1
  507.0 1.3 slice-done.2
  508.2 6.9 multiply_convert_fusion
  515.1 2.0 multiply_convert_fusion.9
  517.2 1.8 convert_reduce_fusion.5
  518.9 3.1 convert_reduce_fusion.4
  522.1 3.0 bitcast_convert_fusion
  525.1 2.4 copy.112
  527.5 2.3 copy.121
  530.1 6.8 convolution_bitcast_fusion
  537.0 7.7 fusion.22
  544.7 8.5 reduce-scatter.15.cloned.1.call-done
  553.2 2.0 reshape.198
  555.2 1.3 copy.109
  556.5 59.3 %reduce-scatter.19.cloned.1.call-done = bf16[128,3072]{1,0:T(8,128)(2,1)} async-done(((bf16[512,3072]{1,0:T(8,128)(2,1)}), bf16[128,3072]{1,0:T(8,128)(2,1)}) %reduce-scatter.19.cloned.1.call-update) | async-done | bytes 786448
  615.8 2.7 reshape.202
  618.5 1.6 copy.113
  620.1 2.8 convert_reduce_fusion.1
  623.0 2.8 fusion.28
  625.8 3.5 convert_reduce_fusion.7
  630.2 1.2 pad_maximum_fusion.2
  631.6 4.0 convolution_bitcast_fusion.1
  635.6 5.3 fusion.32
  641.7 14.1 %all-reduce.1 = (f32[2,192]{1,0:T(2,128)}, f32[768]{0:T(1024)}) all-reduce(f32[2,192]{1,0:T(2,128)S(1)} %pad_maximum_fusion.7, f32[768]{0:T(1024)S(1)} %copy-done.64), channel_id=1, replica_groups=mesh['wide'=8,'narrow'=4] {'wide'}, use_global_device_ids=true, to_apply=%region_29.30 | all-reduce | flops 1152 | bytes 9216 | tf_op jit(solution)/shard_map/psum | solution.py:214
  657.2 40.7 %all-reduce = (f32[2,768]{1,0:T(2,128)}, f32[768]{0:T(1024)}, f32[768]{0:T(1024)}, f32[768]{0:T(1024)}, f32[768]{0:T(1024)}, /*index=5*/f32[768]{0:T(1024)}, f32[768]{0:T(1024)}) all-reduce(f32[2,768]{1,0:T(2,128)S(1)} %pad_maximum_fusion.5, f32[768]{0:T(1024)S(1)} %copy-done.56, ...), channel_id=1, replica_groups=mesh['wide'=8,'narrow'=4] {'wide','narrow'}, use_global_device_ids=true, to_apply=%region_21.22 | all-reduce | flops 6144 | bytes 49152 | tf_op jit(solution)/shard_map/psum | solution.py:201
  697.9 1.5 fusion.12
  699.4 64.8 %all-reduce.6.cloned.1.call-done = f32[2,256,768]{1,2,0:T(8,128)} async-done(((f32[2,256,768]{1,2,0:T(8,128)}), f32[2,256,768]{1,2,0:T(8,128)}) %all-reduce.6.cloned.1.call-update) | async-done | bytes 1572880 | tf_op jit(solution)/shard_map/psum | solution.py:201
  764.2 3.0 copy.85
  767.2 113.3 %all-reduce.8.cloned.1.call-done = (f32[768,3,192]{0,2,1:T(8,128)}, f32[192,768]{1,0:T(8,128)}, f32[768,768]{1,0:T(8,128)}, f32[768,768]{1,0:T(8,128)}) async-done(((f32[768,3,192]{0,2,1:T(8,128)}, f32[192,768]{1,0:T(8,128)}, f32[768,768]{1,0:T(8,128)}, f32[768,768]{1,0:T(8,128)}), (f32[768,3,192]{0,2,1:T(8,128)}, f32[192,768]{1,0:T(8,128)}, f32[768,768]{1,0:T(8,128)}, ...) | async-done | bytes 7077904 | tf_op jit(solution)/shard_map/psum | solution.py:214
  880.5 2.9 copy.127
  884.3 1.4 copy.129
  886.8 1.4 copy.130
  (217 shorter events, 21.5 us)
Async XLA Ops:
  7.2 277.9 %copy-start = (bf16[768,768]{1,0:T(8,128)(2,1)S(1)}, bf16[768,768]{1,0:T(8,128)(2,1)}, u32[]{:S(2)}) copy-start(bf16[768,768]{1,0:T(8,128)(2,1)} %param.29) | copy-start | bytes 3538948
  7.2 74.3 %all-gather.5.cloned.1.call-start = ((), (), s32[]{:S(2)}) async-start(), calls=%async_computation.4 | async-start | bytes 3932160 | tf_op jit(solution)/shard_map/all_gather | solution.py:102
  8.0 4.3 copy-start.69
  10.1 3.9 copy-start.39
  10.1 3.9 copy-start.61
  12.3 69.2 %copy-start.74 = (bf16[768,3,192]{0,2,1:T(8,128)(2,1)S(1)}, bf16[768,3,192]{0,2,1:T(8,128)(2,1)}, u32[]{:S(2)}) copy-start(bf16[768,3,192]{0,2,1:T(8,128)(2,1)} %param.23) | copy-start | bytes 2654212
  15.2 144.7 %reduce-scatter.13.cloned.1.call-start = ((), (), s32[]{:S(2)}) async-start(), calls=%async_computation.9 | async-start | bytes 3932160
  85.6 4.0 copy-start.5
  87.5 4.5 copy-start.2
  89.7 4.8 copy-start.24
  101.2 62.1 %copy-start.67 = (f32[768]{0:T(1024)S(1)}, f32[768]{0:T(1024)}, u32[]{:S(2)}) copy-start(f32[768]{0:T(1024)} %param.26) | copy-start | bytes 9220
  101.2 183.9 %all-gather.9.cloned.1.call-start = ((), (), s32[]{:S(2)}) async-start(), calls=%async_computation.6 | async-start | bytes 7864320 | tf_op jit(solution)/shard_map/all_gather | solution.py:12
  102.7 65.1 %copy-start.7 = (bf16[4,128,768]{1,2,0:T(8,128)(2,1)}, bf16[4,128,768]{1,2,0:T(8,128)(2,1)S(1)}, u32[]{:S(2)}) copy-start(bf16[4,128,768]{1,2,0:T(8,128)(2,1)S(1)} %copy.65) | copy-start | bytes 2359300
  170.2 193.1 %reduce-scatter.17.cloned.1.call-start = ((), (), s32[]{:S(2)}) async-start(), calls=%async_computation.11 | async-start | bytes 3932160
  171.0 118.8 %copy-start.65 = (f32[768]{0:T(1024)}, f32[768]{0:T(1024)S(1)}, u32[]{:S(2)}) copy-start(f32[768]{0:T(1024)S(1)} %dynamic_slice.3) | copy-start | bytes 9220
  285.1 4.8 copy-start.72
  285.1 4.8 copy-start.73
  289.9 7.0 copy-start.77
  304.6 124.1 %all-gather.7.cloned.1.call-start = ((), (), s32[]{:S(2)}) async-start(), calls=%async_computation.5 | async-start | bytes 3932160 | tf_op jit(solution)/shard_map/all_gather | solution.py:115
  305.2 187.1 %all-gather.11.cloned.1.call-start = ((), (), s32[]{:S(2)}) async-start(), calls=%async_computation.7 | async-start | bytes 3932160 | tf_op jit(solution)/shard_map/all_gather | solution.py:139
  367.6 4.0 copy-start.8
  367.6 4.0 copy-start.41
  369.5 4.3 copy-start.44
  373.9 179.3 %reduce-scatter.15.cloned.1.call-start = ((), (), s32[]{:S(2)}) async-start(), calls=%async_computation.10 | async-start | bytes 3932160
  444.6 47.6 %copy-start.23 = (bf16[192,768]{1,0:T(8,128)(2,1)S(1)}, bf16[192,768]{1,0:T(8,128)(2,1)}, u32[]{:S(2)}) copy-start(bf16[192,768]{1,0:T(8,128)(2,1)} %param.25) | copy-start | bytes 884740
  444.7 50.3 %copy-start.6 = (bf16[1,4,512,192]{2,3,0,1:T(8,128)(2,1)S(1)}, bf16[1,4,512,192]{2,3,0,1:T(8,128)(2,1)}, u32[]{:S(2)}) copy-start(bf16[1,4,512,192]{2,3,0,1:T(8,128)(2,1)} %copy-done.5) | copy-start | bytes 2359300
  444.7 50.3 %copy-start.25 = (f32[4,3,512]{2,1,0:T(4,128)S(1)}, f32[4,3,512]{2,1,0:T(4,128)}, u32[]{:S(2)}) copy-start(f32[4,3,512]{2,1,0:T(4,128)} %copy-done.24) | copy-start | bytes 73732
  444.7 171.1 %reduce-scatter.19.cloned.1.call-start = ((), (), s32[]{:S(2)}) async-start(), calls=%async_computation.12 | async-start | bytes 3932160
  494.9 10.7 %slice-start = ((s8[12582912]{0:T(1024)(128)(4,1)}), s8[4194304]{0:T(1024)(128)(4,1)S(1)}, s32[]{:S(2)}) async-start(s8[12582912]{0:T(1024)(128)(4,1)} %bitcast.156), calls=%async_computation.14 | async-start | bytes 8388608
  495.0 12.0 %slice-start.1 = ((s8[12582912]{0:T(1024)(128)(4,1)}), s8[4194304]{0:T(1024)(128)(4,1)S(1)}, s32[]{:S(2)}) async-start(s8[12582912]{0:T(1024)(128)(4,1)} %bitcast.156), calls=%async_computation.15 | async-start | bytes 8388608
  495.0 13.3 %slice-start.2 = ((s8[12582912]{0:T(1024)(128)(4,1)}), s8[4194304]{0:T(1024)(128)(4,1)S(1)}, s32[]{:S(2)}) async-start(s8[12582912]{0:T(1024)(128)(4,1)} %bitcast.156), calls=%async_computation.16 | async-start | bytes 8388608
  508.2 6.9 copy-start.11
  517.1 5.0 copy-start.20
  529.9 7.1 copy-start.66
  529.9 234.3 %all-reduce.6.cloned.1.call-start = ((), (), s32[]{:S(2)}) async-start(), calls=%async_computation.8 | async-start | bytes 3145728 | tf_op jit(solution)/shard_map/psum | solution.py:201
  618.5 4.5 copy-start.49
  618.5 4.5 copy-start.47
  620.1 5.7 copy-start.4
  620.1 5.7 copy-start.9
  620.1 5.7 copy-start.17
  620.1 5.7 copy-start.42
  620.1 5.7 copy-start.45
  620.1 5.7 copy-start.52
  620.1 5.7 copy-start.63
  625.8 3.5 copy-start.70
  625.8 3.5 copy-start.76
  631.4 4.2 copy-start.21
  631.5 4.2 copy-start.29
  631.5 4.1 copy-start.32
  631.5 249.0 %all-reduce.8.cloned.1.call-start = ((), (), s32[]{:S(2)}) async-start(), calls=%async_computation.13 | async-start | bytes 14155776 | tf_op jit(solution)/shard_map/psum | solution.py:214
  640.9 14.9 %copy-start.43 = (f32[4,768]{1,0:T(4,128)S(1)}, f32[4,768]{1,0:T(4,128)}, u32[]{:S(2)}) copy-start(f32[4,768]{1,0:T(4,128)} %get-tuple-element.77) | copy-start | bytes 36868
  640.9 14.9 %copy-start.71 = (pred[4]{0:T(512)(128)(4,1)S(1)}, pred[4]{0:T(512)(128)(4,1)}, u32[]{:S(2)}) copy-start(pred[4]{0:T(512)(128)(4,1)} %copy-done.69) | copy-start | bytes 16
  640.9 15.0 %copy-start.16 = (bf16[4,128,768]{1,2,0:T(8,128)(2,1)S(1)}, bf16[4,128,768]{1,2,0:T(8,128)(2,1)}, u32[]{:S(2)}) copy-start(bf16[4,128,768]{1,2,0:T(8,128)(2,1)} %get-tuple-element.84) | copy-start | bytes 2359300
  641.0 16.2 %copy-start.53 = (f32[768]{0:T(1024)S(1)}, f32[768]{0:T(1024)}, u32[]{:S(2)}) copy-start(f32[768]{0:T(1024)} %get-tuple-element.54) | copy-start | bytes 9220
  641.0 16.2 %copy-start.54 = (f32[768]{0:T(1024)S(1)}, f32[768]{0:T(1024)}, u32[]{:S(2)}) copy-start(f32[768]{0:T(1024)} %get-tuple-element.50) | copy-start | bytes 9220
  641.0 16.2 %copy-start.55 = (f32[768]{0:T(1024)S(1)}, f32[768]{0:T(1024)}, u32[]{:S(2)}) copy-start(f32[768]{0:T(1024)} %get-tuple-element.56) | copy-start | bytes 9220
  641.0 16.2 %copy-start.56 = (f32[768]{0:T(1024)S(1)}, f32[768]{0:T(1024)}, u32[]{:S(2)}) copy-start(f32[768]{0:T(1024)} %get-tuple-element.52) | copy-start | bytes 9220
  641.0 16.2 %copy-start.57 = (f32[768]{0:T(1024)S(1)}, f32[768]{0:T(1024)}, u32[]{:S(2)}) copy-start(f32[768]{0:T(1024)} %get-tuple-element.85) | copy-start | bytes 9220
  641.0 16.2 %copy-start.58 = (f32[768]{0:T(1024)S(1)}, f32[768]{0:T(1024)}, u32[]{:S(2)}) copy-start(f32[768]{0:T(1024)} %get-tuple-element.75) | copy-start | bytes 9220
  641.0 56.9 %copy-start.27 = (bf16[4,128,768]{1,2,0:T(8,128)(2,1)S(1)}, bf16[4,128,768]{1,2,0:T(8,128)(2,1)}, u32[]{:S(2)}) copy-start(bf16[4,128,768]{1,2,0:T(8,128)(2,1)} %copy-done.26) | copy-start | bytes 2359300
  641.0 56.9 %copy-start.35 = (bf16[256,768]{1,0:T(8,128)(2,1)S(1)}, bf16[256,768]{1,0:T(8,128)(2,1)}, u32[]{:S(2)}) copy-start(bf16[256,768]{1,0:T(8,128)(2,1)} %copy-done.34) | copy-start | bytes 1179652
  641.0 56.8 %copy-start.37 = (bf16[256,768]{1,0:T(8,128)(2,1)S(1)}, bf16[256,768]{1,0:T(8,128)(2,1)}, u32[]{:S(2)}) copy-start(bf16[256,768]{1,0:T(8,128)(2,1)} %copy-done.36) | copy-start | bytes 1179652
  880.5 3.8 copy-start.19
  884.3 3.9 copy-start.1
  (28 other events, 54.0 us)
Sparse Core Ops, SparseCore 0:
  15.3 66.1 all-gather.4
  101.3 58.5 reduce-scatter.12
  170.3 114.7 all-gather.8
  304.7 58.5 reduce-scatter.16
  365.3 63.2 all-gather.6
  430.6 61.5 all-gather.10
  494.6 58.5 reduce-scatter.14
  555.5 60.2 reduce-scatter.18
  631.6 132.5 all-reduce.5
  768.9 111.5 all-reduce.7
